TPU v7x, 32 devices: a whole 2x2x4 slice. The times are simulated.
32 devices in a mesh: grp: 2 (over x), tile: 8 (over z, y), wave: 2 (over core).
Axes of the slice: x: 2, y: 2, z: 4, core: 2. Of those that a mesh axis runs over, the one named last changes fastest.
Arguments:
- residual: float32 [16, 8, 2, 8, 128], P(('grp', 'tile'), 'wave'), parts along dimension 0, may hold values from -210 to 210
- kernel: bfloat16 [16, 8, 9, 2, 128, 128], P(('grp', 'tile'), 'wave'), parts along dimension 0, may hold values from -0.125 to 0.125
- offsets: float32 [16, 8, 2, 128], P(('grp', 'tile'), 'wave'), parts along dimension 0, may hold values from 0 to 1
- neighbor: int32 [16, 8, 9], P(('grp', 'tile'), 'wave'), parts along dimension 0, may hold values from 0 to 8, each once within a row
- frequency: int32 [16], P('grp'), parts along dimension 0, may hold values from 0 to 7, each once
- lattice_x: int32 [128], replicated, may hold values from 0 to 127, each once
- lattice_y: int32 [128], replicated, may hold values from 0 to 127, each once
- spectral_weight: float32 [8, 128, 128], replicated, may hold values from 0.1 to 3
Outputs:
- image_two: float32 [16, 8, 2, 8, 128], P(('grp', 'tile'), 'wave'), parts along dimension 0
- arnoldi: float32 [8, 8], P('grp'), parts along dimension 0
There are 2 independent parts, one for each index of `grp`. A program takes and returns all parts, laid end to end along the dimension named above; an argument that names none is the same for every part. Nothing has to cross between parts.
Inputs may be any that keep to these rules, and one draw needn't show every extreme that they name: `neighbor`: each row names each of the nine neighbour slots once. `frequency`: each index appears once. `lattice_x`: each index appears once. `lattice_y`: each index appears once.
All inputs are finite; a program needn't handle non-finite values.
Results may differ from a plain program's by a relative error of at most 0.013.
Values may be sent and summed in bfloat16 or wider, within the bound.
A program may use at most 64 MiB of HBM per device.

v0:
```python
import math
import jax
import jax.numpy as jnp
from jax import lax
from jax.sharding import PartitionSpec as P

two_pi = 2.0 * math.pi
eps_norm = 1e-06


def padded_2(array, sides, width):
    for axis, dim in sides:
        size, length = (lax.axis_size(axis), array.shape[dim])
        up = [(i, (i + 1) % size) for i in range(size)]
        down = [(j, i) for i, j in up]
        last = lax.slice_in_dim(array, length - width, length, axis=dim)
        initial = lax.slice_in_dim(array, 0, width, axis=dim)
        before = lax.ppermute(last, axis, up)
        after = lax.ppermute(initial, axis, down)
        array = jnp.concatenate([before, array, after], axis=dim)
    return array


def phase_table(position, harmonic):
    phase_angle = two_pi * (position[:, None] * harmonic[None, :])
    return (jnp.cos(phase_angle).astype(jnp.bfloat16), jnp.sin(phase_angle).astype(jnp.bfloat16))


def project_rows(cosine_cols, sine_cols, twisted):
    row_count = cosine_cols.shape[1]
    stacked = jnp.concatenate([cosine_cols, sine_cols], 1)
    gram_matrix = lax.dot_general(
        stacked, twisted, (((0,), (0,)), ((), ())), preferred_element_type=jnp.float32
    )
    gram_matrix = gram_matrix.reshape(2, row_count, 2, -1)
    coef_real = gram_matrix[0, :, 0] + gram_matrix[1, :, 1]
    coef_imag = gram_matrix[0, :, 1] - gram_matrix[1, :, 0]
    return jnp.stack([coef_real, coef_imag], 1)


def expand_rows(cosine_cols, sine_cols, scaled):
    row_count = scaled.shape[0]
    upper_rows = scaled.reshape(row_count, -1)
    lower_rows = jnp.stack([-scaled[:, 1], scaled[:, 0]], 1).reshape(row_count, -1)
    matrix = jnp.concatenate([upper_rows, lower_rows], 0)
    stacked = jnp.concatenate([cosine_cols, sine_cols], 1)
    return jnp.dot(stacked, matrix, preferred_element_type=jnp.float32)


def twist_density(panel_density, cosine_y, sine_y):
    density_real = panel_density[:, 0, :, None].astype(jnp.float32)
    density_imag = panel_density[:, 1, :, None].astype(jnp.float32)
    wave_cos = cosine_y.astype(jnp.float32)[:, None, :]
    wave_sin = sine_y.astype(jnp.float32)[:, None, :]
    part_real = wave_cos * density_real + wave_sin * density_imag
    part_imag = wave_cos * density_imag - wave_sin * density_real
    return (
        jnp.stack([part_real, part_imag], 1)
        .reshape(panel_density.shape[0], -1)
        .astype(jnp.bfloat16)
    )


def finish(summed, cosine_y, sine_y, vectors):
    shaped = summed.reshape(summed.shape[0], 2, vectors, -1)
    wave_cos = cosine_y.astype(jnp.float32)[:, None, :]
    wave_sin = sine_y.astype(jnp.float32)[:, None, :]
    far_real = jnp.sum(shaped[:, 0] * wave_cos - shaped[:, 1] * wave_sin, -1)
    far_imag = jnp.sum(shaped[:, 0] * wave_sin + shaped[:, 1] * wave_cos, -1)
    return jnp.stack([far_real, far_imag], 1)


def combine_near(product, vectors):
    first_half = product[:, 0]
    second = product[:, 1]
    near_real = first_half[:, :vectors] - second[:, vectors:]
    near_imag = second[:, :vectors] + first_half[:, vectors:]
    return jnp.stack([near_real, near_imag], 1)


def panel_sum(values):
    return jnp.sum(values, axis=(0, 1, 3))


def per_device(
    residual, kernel, offsets, neighbor, frequency, lattice_x, lattice_y, spectral_weight
):
    strips = residual.shape[0]
    tiles_y = residual.shape[1]
    vectors = residual.shape[3]
    panels_t = residual.shape[4]
    modes_x = spectral_weight.shape[1]
    modes_y = spectral_weight.shape[2]
    count_x = lax.axis_size("tile") * strips
    count_y = lax.axis_size("wave") * tiles_y
    devices = lax.axis_size("tile") * lax.axis_size("wave")
    panels = count_x * count_y * panels_t
    local_rows = strips * tiles_y * panels_t
    column = (lax.axis_index("tile") * strips + jnp.arange(strips)).astype(jnp.float32)
    row_index = (lax.axis_index("wave") * tiles_y + jnp.arange(tiles_y)).astype(jnp.float32)
    position_x = ((column[:, None, None] + offsets[:, :, 0, :]) / count_x).reshape(-1)
    position_y = ((row_index[None, :, None] + offsets[:, :, 1, :]) / count_y).reshape(-1)
    harmonic_x = (lattice_x - modes_x // 2).astype(jnp.float32)
    harmonic_y = (lattice_y - modes_y // 2).astype(jnp.float32)
    cosine_x, sine_x = phase_table(position_x, harmonic_x)
    cosine_y, sine_y = phase_table(position_y, harmonic_y)
    weight_rows = jnp.take(spectral_weight, frequency, axis=0)
    factor = weight_rows * (1.0 / math.sqrt(modes_x * modes_y * panels))
    factor_wide = jnp.transpose(factor, (1, 0, 2)).reshape(modes_x, vectors * modes_y)[:, None, :]

    def near_field(density):
        padded = padded_2(density, (("tile", 0), ("wave", 1)), 1)
        candidates = []
        for slot_index in range(9):
            shift_x = slot_index // 3 - 1
            shift_y = slot_index % 3 - 1
            candidates.append(
                padded[1 + shift_x : 1 + shift_x + strips, 1 + shift_y : 1 + shift_y + tiles_y]
            )
        stacked = jnp.stack(candidates, 2).reshape(strips * tiles_y, 9, -1)
        picked = jnp.take_along_axis(stacked, neighbor.reshape(strips * tiles_y, 9, 1), axis=1)
        picked = picked.reshape(strips * tiles_y, 9, 2 * vectors, panels_t)
        blocks = kernel.reshape(strips * tiles_y, 9, 2, panels_t, panels_t)
        product = jnp.einsum("tjmp,tjcpq->tcmq", picked, blocks, preferred_element_type=jnp.float32)
        return combine_near(product, vectors).reshape(strips, tiles_y, 2, vectors, panels_t)

    def far_field(density):
        panel_density = jnp.transpose(density, (0, 1, 4, 2, 3)).reshape(local_rows, 2, vectors)
        twisted = twist_density(panel_density, cosine_y, sine_y)
        partial_coeffs = project_rows(cosine_x, sine_x, twisted)
        share_rows = modes_x // devices
        shares = lax.psum_scatter(partial_coeffs, ("tile", "wave"), scatter_dimension=0, tiled=True)
        owner_index = lax.axis_index("tile") * lax.axis_size("wave") + lax.axis_index("wave")
        owner_factor = lax.dynamic_slice_in_dim(
            factor_wide, owner_index * share_rows, share_rows, 0
        )
        owner_scaled = (shares * owner_factor).astype(jnp.bfloat16)
        scaled = lax.all_gather(owner_scaled, ("tile", "wave"), axis=0, tiled=True)
        summed = expand_rows(cosine_x, sine_x, scaled)
        far_panel = finish(summed, cosine_y, sine_y, vectors)
        return far_panel.reshape(strips, tiles_y, panels_t, 2, vectors).transpose(0, 1, 3, 4, 2)

    def apply_operator(density):
        return 0.5 * density.astype(jnp.float32) + near_field(density) + far_field(density)

    local_sq = panel_sum(
        residual[:, :, 0] * residual[:, :, 0] + residual[:, :, 1] * residual[:, :, 1]
    )
    squares = lax.psum(local_sq, ("tile", "wave"))
    basis_scale = jnp.sqrt(squares / panels + eps_norm)
    basis_one = (residual / basis_scale[None, None, None, :, None]).astype(jnp.bfloat16)
    image_one = apply_operator(basis_one)
    basis_real = basis_one[:, :, 0].astype(jnp.float32)
    basis_imag = basis_one[:, :, 1].astype(jnp.float32)
    image_real = image_one[:, :, 0]
    image_imag = image_one[:, :, 1]
    inner_real, inner_imag = lax.psum(
        (
            panel_sum(basis_real * image_real + basis_imag * image_imag),
            panel_sum(basis_real * image_imag - basis_imag * image_real),
        ),
        ("tile", "wave"),
    )
    coef_real = inner_real / panels
    coef_imag = inner_imag / panels
    wide_real = coef_real[None, None, :, None]
    wide_imag = coef_imag[None, None, :, None]
    update_real = image_real - (wide_real * basis_real - wide_imag * basis_imag)
    update_imag = image_imag - (wide_real * basis_imag + wide_imag * basis_real)
    update_sq = lax.psum(
        panel_sum(update_real * update_real + update_imag * update_imag), ("tile", "wave")
    )
    update_scale = jnp.sqrt(update_sq / panels + eps_norm)
    next_basis = (
        jnp.stack([update_real, update_imag], 2) / update_scale[None, None, None, :, None]
    ).astype(jnp.bfloat16)
    image_two = apply_operator(next_basis)
    arnoldi = jnp.stack([basis_scale, coef_real, coef_imag, update_scale])
    return (image_two, arnoldi)


def solution(mesh):
    return jax.shard_map(
        per_device,
        mesh=mesh,
        in_specs=(
            P(("grp", "tile"), "wave", None, None, None),
            P(("grp", "tile"), "wave", None, None, None, None),
            P(("grp", "tile"), "wave", None, None),
            P(("grp", "tile"), "wave", None),
            P("grp"),
            P(),
            P(),
            P(),
        ),
        out_specs=(P(("grp", "tile"), "wave", None, None, None), P("grp", None)),
        check_vma=False,
    )
```

profile of v0, /device:TPU:0, one launch (start us, length us, event | category | flops | bytes accessed | tf_op | source)
XLA Modules:
  0.0 307.0 jit_solution(9363511399105179548)
XLA Ops:
  8.2 34.9 %psum.28 = f32[8]{0:T(128)S(1)} all-reduce(f32[8]{0:T(128)S(1)} %add_reduce_fusion.2), channel_id=1, replica_groups=mesh['grp'=2,'tile'=8,'wave'=2] {'tile','wave'}, use_global_device_ids=true, to_apply=%region_1.2 | all-reduce | flops 8 | bytes 64 | tf_op jit(solution)/shard_map/psum | solution.py:149
  43.7 1.4 fusion.22
  45.2 4.7 %collective-permute-start.1 = (bf16[1,4,2,8,128]{4,3,1,2,0:T(8,128)(2,1)}, bf16[1,4,2,8,128]{4,3,1,2,0:T(8,128)(2,1)}, u32[]{:S(2)}, u32[]{:S(2)}) collective-permute-start(bf16[1,4,2,8,128]{4,3,1,2,0:T(8,128)(2,1)} %fusion.22), channel_id=1, source_target_pairs={{2,0},{4,2},{6,4},{8,6},{10,8},{12,10},{14,12},{0,14},{3,1},{5,3},... | collective-permute-start | bytes 49160 | tf_op jit(solution)/shard_map/ppermute | solution.py:19
  54.7 1.1 cosine_convert_fusion.1
  56.9 1.1 pad_maximum_fusion.2
  58.7 1.6 gather_fusion
  61.7 1.2 copy.121
  63.0 1.3 pad_maximum_fusion.31
  67.8 1.2 copy.122
  73.7 1.5 gather_fusion.1
  76.5 36.3 %reduce-scatter.3.cloned.1.call-done = f32[8,2,1024]{2,0,1:T(8,128)} async-done(((f32[128,2,1024]{2,0,1:T(8,128)}), f32[8,2,1024]{2,0,1:T(8,128)}) %reduce-scatter.3.cloned.1.call-update) | async-done | bytes 65552 | tf_op jit(solution)/shard_map/reduce_scatter | solution.py:132
  113.7 20.8 %all_gather.6 = bf16[128,2,1024]{2,0,1:T(8,128)(2,1)S(1)} all-gather(bf16[8,2,1024]{2,0,1:T(8,128)(2,1)S(1)} %multiply_convert_fusion.1), channel_id=1, replica_groups=mesh['grp'=2,'tile'=8,'wave'=2] {'tile','wave'}, dimensions={0}, use_global_device_ids=true | all-gather | bytes 557056 | tf_op jit(solution)/shard_map/all_gather | solution.py:138
  136.3 1.1 pad_maximum_fusion.4
  138.4 2.0 convolution_bitcast_fusion.1
  141.4 1.2 subtract_reduce_fusion.1
  145.2 29.8 %all-reduce = (f32[8]{0:T(128)S(1)}, f32[8]{0:T(128)S(1)}) all-reduce(f32[8]{0:T(128)S(1)} %get-tuple-element.16, f32[8]{0:T(128)S(1)} %get-tuple-element.15), channel_id=1, replica_groups=mesh['grp'=2,'tile'=8,'wave'=2] {'tile','wave'}, use_global_device_ids=true, to_apply=%region_8.10 | all-reduce | flops 16 | bytes 128 | tf_op jit(solution)/shard_map/psum | solution.py:157
  176.7 29.5 %psum.31 = f32[8]{0:T(128)S(1)} all-reduce(f32[8]{0:T(128)S(1)} %fusion.40), channel_id=1, replica_groups=mesh['grp'=2,'tile'=8,'wave'=2] {'tile','wave'}, use_global_device_ids=true, to_apply=%region_10.12 | all-reduce | flops 8 | bytes 64 | tf_op jit(solution)/shard_map/psum | solution.py:170
  206.4 4.7 %collective-permute-start.5 = (bf16[1,4,2,8,128]{4,3,1,2,0:T(8,128)(2,1)S(1)}, bf16[1,4,2,8,128]{4,3,1,2,0:T(8,128)(2,1)S(1)}, u32[]{:S(2)}, u32[]{:S(2)}) collective-permute-start(bf16[1,4,2,8,128]{4,3,1,2,0:T(8,128)(2,1)S(1)} %fusion.20), channel_id=1, source_target_pairs={{2,0},{4,2},{6,4},{8,6},{10,8},{12,10},{14,12},{0,14},{3,1},{5,3},... | collective-permute-start | bytes 49160 | tf_op jit(solution)/shard_map/ppermute | solution.py:19
  213.7 1.1 pad_maximum_fusion.3
  217.2 1.5 gather_fusion.2
  219.4 50.2 %reduce-scatter.5.cloned.1.call-done = f32[8,2,1024]{2,0,1:T(8,128)} async-done(((f32[128,2,1024]{2,0,1:T(8,128)}), f32[8,2,1024]{2,0,1:T(8,128)}) %reduce-scatter.5.cloned.1.call-update) | async-done | bytes 65552 | tf_op jit(solution)/shard_map/reduce_scatter | solution.py:132
  270.5 20.8 %all_gather.7 = bf16[128,2,1024]{2,0,1:T(8,128)(2,1)S(1)} all-gather(bf16[8,2,1024]{2,0,1:T(8,128)(2,1)S(1)} %multiply_convert_fusion), channel_id=1, replica_groups=mesh['grp'=2,'tile'=8,'wave'=2] {'tile','wave'}, dimensions={0}, use_global_device_ids=true | all-gather | bytes 557056 | tf_op jit(solution)/shard_map/all_gather | solution.py:138
  295.1 2.0 convolution_bitcast_fusion
  298.1 1.2 subtract_reduce_fusion
  (197 shorter events, 39.9 us)
Async XLA Ops:
  7.2 68.3 %copy-start = (bf16[1,4,9,2,128,128]{5,4,3,2,1,0:T(8,128)(2,1)S(1)}, bf16[1,4,9,2,128,128]{5,4,3,2,1,0:T(8,128)(2,1)}, u32[]{:S(2)}) copy-start(bf16[1,4,9,2,128,128]{5,4,3,2,1,0:T(8,128)(2,1)} %param.11) | copy-start | bytes 7077892
  7.2 105.6 %reduce-scatter.3.cloned.1.call-start = ((), (), s32[]{:S(2)}) async-start(), calls=%async_computation.2 | async-start | bytes 1114112 | tf_op jit(solution)/shard_map/reduce_scatter | solution.py:132
  43.7 7.0 %copy-start.19 = (f32[8]{0:T(128)}, f32[8]{0:T(128)S(1)}, u32[]{:S(2)}) copy-start(f32[8]{0:T(128)S(1)} %get-tuple-element.68) | copy-start | bytes 100
  45.2 17.8 %collective-permute-start = (bf16[1,4,2,8,128]{4,3,1,2,0:T(8,128)(2,1)}, bf16[1,4,2,8,128]{4,3,1,2,0:T(8,128)(2,1)}, u32[]{:S(2)}, u32[]{:S(2)}) collective-permute-start(bf16[1,4,2,8,128]{4,3,1,2,0:T(8,128)(2,1)} %fusion.22), channel_id=1, source_target_pairs={{0,2},{2,4},{4,6},{6,8},{8,10},{10,12},{12,14},{14,0},{1,3},{3,5},... | collective-permute-start | bytes 49160 | tf_op jit(solution)/shard_map/ppermute | solution.py:18
  45.2 17.8 %collective-permute-start.1 = (bf16[1,4,2,8,128]{4,3,1,2,0:T(8,128)(2,1)}, bf16[1,4,2,8,128]{4,3,1,2,0:T(8,128)(2,1)}, u32[]{:S(2)}, u32[]{:S(2)}) collective-permute-start(bf16[1,4,2,8,128]{4,3,1,2,0:T(8,128)(2,1)} %fusion.22), channel_id=1, source_target_pairs={{2,0},{4,2},{6,4},{8,6},{10,8},{12,10},{14,12},{0,14},{3,1},{5,3},... | collective-permute-start | bytes 49160 | tf_op jit(solution)/shard_map/ppermute | solution.py:19
  53.9 12.3 %copy-start.1 = (f32[512,128]{0,1:T(8,128)}, f32[512,128]{0,1:T(8,128)S(1)}, u32[]{:S(2)}) copy-start(f32[512,128]{0,1:T(8,128)S(1)} %get-tuple-element.64) | copy-start | bytes 786436
  58.0 211.7 %reduce-scatter.5.cloned.1.call-start = ((), (), s32[]{:S(2)}) async-start(), calls=%async_computation.3 | async-start | bytes 1114112 | tf_op jit(solution)/shard_map/reduce_scatter | solution.py:132
  64.3 7.5 %collective-permute-start.2 = (bf16[3,1,2,8,128]{4,3,1,2,0:T(8,128)(2,1)}, bf16[3,1,2,8,128]{4,3,1,2,0:T(8,128)(2,1)}, u32[]{:S(2)}, u32[]{:S(2)}) collective-permute-start(bf16[3,1,2,8,128]{4,3,1,2,0:T(8,128)(2,1)} %get-tuple-element.56), channel_id=1, source_target_pairs={{0,1},{1,0},{2,3},{3,2},{4,5},{5,4},{6,7},{7,6},{8,9},{9,8},{10,11... | collective-permute-start | bytes 36872 | tf_op jit(solution)/shard_map/ppermute | solution.py:18
  67.7 7.5 %copy-start.21 = (pred[4,9]{1,0:T(4,128)(4,1)S(1)}, pred[4,9]{1,0:T(4,128)(4,1)}, u32[]{:S(2)}) copy-start(pred[4,9]{1,0:T(4,128)(4,1)} %and_bitcast_fusion) | copy-start | bytes 112
  69.0 43.9 %copy-start.16 = (f32[8,1,1024]{2,0,1:T(8,128)}, f32[8,1,1024]{2,0,1:T(8,128)S(1)}, u32[]{:S(2)}) copy-start(f32[8,1,1024]{2,0,1:T(8,128)S(1)} %copy.122) | copy-start | bytes 98308
  70.5 2.1 collective-permute-start.3
  134.4 4.0 %copy-start.10 = (bf16[512,128]{0,1:T(8,128)(2,1)S(1)}, bf16[512,128]{0,1:T(8,128)(2,1)}, u32[]{:S(2)}) copy-start(bf16[512,128]{0,1:T(8,128)(2,1)} %copy-done.9) | copy-start | bytes 393220
  141.4 2.0 copy-start.20
  141.4 69.8 %copy-start.2 = (f32[512,128]{0,1:T(8,128)S(1)}, f32[512,128]{0,1:T(8,128)}, u32[]{:S(2)}) copy-start(f32[512,128]{0,1:T(8,128)} %copy-done.1) | copy-start | bytes 786436
  176.7 38.0 %copy-start.12 = (f32[1,4,1,8,128]{4,3,1,2,0:T(8,128)}, f32[1,4,1,8,128]{4,3,1,2,0:T(8,128)S(1)}, u32[]{:S(2)}) copy-start(f32[1,4,1,8,128]{4,3,1,2,0:T(8,128)S(1)} %get-tuple-element.51) | copy-start | bytes 49156
  176.7 38.0 %copy-start.14 = (f32[1,4,1,8,128]{4,3,1,2,0:T(8,128)}, f32[1,4,1,8,128]{4,3,1,2,0:T(8,128)S(1)}, u32[]{:S(2)}) copy-start(f32[1,4,1,8,128]{4,3,1,2,0:T(8,128)S(1)} %get-tuple-element.52) | copy-start | bytes 49156
  206.4 8.4 %collective-permute-start.4 = (bf16[1,4,2,8,128]{4,3,1,2,0:T(8,128)(2,1)S(1)}, bf16[1,4,2,8,128]{4,3,1,2,0:T(8,128)(2,1)S(1)}, u32[]{:S(2)}, u32[]{:S(2)}) collective-permute-start(bf16[1,4,2,8,128]{4,3,1,2,0:T(8,128)(2,1)S(1)} %fusion.20), channel_id=1, source_target_pairs={{0,2},{2,4},{4,6},{6,8},{8,10},{10,12},{12,14},{14,0},{1,3},{3,5},... | collective-permute-start | bytes 49160 | tf_op jit(solution)/shard_map/ppermute | solution.py:18
  206.4 8.4 %collective-permute-start.5 = (bf16[1,4,2,8,128]{4,3,1,2,0:T(8,128)(2,1)S(1)}, bf16[1,4,2,8,128]{4,3,1,2,0:T(8,128)(2,1)S(1)}, u32[]{:S(2)}, u32[]{:S(2)}) collective-permute-start(bf16[1,4,2,8,128]{4,3,1,2,0:T(8,128)(2,1)S(1)} %fusion.20), channel_id=1, source_target_pairs={{2,0},{4,2},{6,4},{8,6},{10,8},{12,10},{14,12},{0,14},{3,1},{5,3},... | collective-permute-start | bytes 49160 | tf_op jit(solution)/shard_map/ppermute | solution.py:19
  214.8 4.0 %copy-start.22 = (pred[4,9]{1,0:T(4,128)(4,1)S(1)}, pred[4,9]{1,0:T(4,128)(4,1)}, u32[]{:S(2)}) copy-start(pred[4,9]{1,0:T(4,128)(4,1)} %and_bitcast_fusion) | copy-start | bytes 112
  214.8 1.2 collective-permute-start.7
  215.5 1.3 collective-permute-start.6
  218.7 51.0 %copy-start.17 = (f32[8,1,1024]{2,0,1:T(8,128)S(1)}, f32[8,1,1024]{2,0,1:T(8,128)}, u32[]{:S(2)}) copy-start(f32[8,1,1024]{2,0,1:T(8,128)} %copy-done.16) | copy-start | bytes 98308
  291.3 3.8 %copy-start.11 = (bf16[512,128]{0,1:T(8,128)(2,1)S(1)}, bf16[512,128]{0,1:T(8,128)(2,1)}, u32[]{:S(2)}) copy-start(bf16[512,128]{0,1:T(8,128)(2,1)} %copy-done.9) | copy-start | bytes 393220
  298.0 1.4 copy-start.15
  (11 other events, 11.5 us)
Sparse Core Ops, SparseCore 0:
  58.1 54.6 reduce-scatter.2
  214.9 54.7 reduce-scatter.4
where the time goes:
time: 308 us; the launch traced here: 307 us
  blocking collectives  136 us (44%)
  waiting for transfers between devices  87.3 us (28%)
  other arithmetic  30 us (10%)
  local copies, waits for them, and re-layouts  22.2 us (7%)
  between operations  14.9 us (5%)
  starting transfers between devices  10.7 us (3%)
  matrix products  6.26 us (2%)
    reduce_scatter x2, waiting for transfers between devices, far_field(): lax.psum_scatter(partial_coeffs, ('tile', 'wave'), scatter_dimension=0, t...  86.5 us
    all_gather x2, blocking collectives, far_field(): scaled = lax.all_gather(owner_scaled, ('tile', 'wave'), axis=0, tiled=True)  41.5 us
    psum x1, blocking collectives, per_device(): squares = lax.psum(local_sq, ('tile', 'wave'))  34.9 us
    psum x1, blocking collectives, per_device(): lax.psum((panel_sum(basis_real * image_real + basis_imag * image_imag), p...  29.8 us
    psum x1, blocking collectives, per_device(): lax.psum(panel_sum(update_real * update_real + update_imag * update_imag)...  29.5 us
    ppermute x4, starting transfers between devices, padded_2(): after = lax.ppermute(initial, axis, down)  10.1 us
  transfers between devices with their start and end apart: 10, of which 3 were waited for; matrix products, arithmetic and copies ran while one was open for 10% of the time, Pallas kernels for 0%

commit v1 on v0

--- a/solution.py
+++ b/solution.py
@@ -167,8 +167,11 @@
     wide_imag = coef_imag[None, None, :, None]
     update_real = image_real - (wide_real * basis_real - wide_imag * basis_imag)
     update_imag = image_imag - (wide_real * basis_imag + wide_imag * basis_real)
-    update_sq = lax.psum(
-        panel_sum(update_real * update_real + update_imag * update_imag), ("tile", "wave")
+    update_sq = jnp.sum(
+        lax.all_gather(
+            panel_sum(update_real * update_real + update_imag * update_imag), ("tile", "wave")
+        ),
+        axis=0,
     )
     update_scale = jnp.sqrt(update_sq / panels + eps_norm)
     next_basis = (

time: 308 us -> 309 us (level)
    psum x1 -> x0, blocking collectives: 29.5 us -> none  [per_device(): lax.psum(panel_sum(update_real * update_real + update_imag * update_imag)...]
    unnamed x0 -> x1, blocking collectives: none -> 29.5 us
  transfers between devices with their start and end apart: 10 -> 10, of which waited for: 3 -> 3; matrix products, arithmetic and copies ran while one was open for 10% -> 11% of each run, Pallas kernels for 0% -> 0%
where the time goes in v1:
time: 309 us; the launch traced here: 307 us
  blocking collectives  136 us (44%)
  waiting for transfers between devices  85.4 us (28%)
  other arithmetic  30.1 us (10%)
  local copies, waits for them, and re-layouts  23.7 us (8%)
  between operations  15.5 us (5%)
  starting transfers between devices  10.7 us (3%)
  matrix products  6.25 us (2%)
    reduce_scatter x2, waiting for transfers between devices, far_field(): lax.psum_scatter(partial_coeffs, ('tile', 'wave'), scatter_dimension=0, t...  84.6 us
    all_gather x2, blocking collectives, far_field(): scaled = lax.all_gather(owner_scaled, ('tile', 'wave'), axis=0, tiled=True)  41.5 us
    psum x1, blocking collectives, per_device(): squares = lax.psum(local_sq, ('tile', 'wave'))  34.9 us
    psum x1, blocking collectives, per_device(): lax.psum((panel_sum(basis_real * image_real + basis_imag * image_imag), p...  29.8 us
    unnamed x1, blocking collectives  29.5 us
    ppermute x4, starting transfers between devices, padded_2(): after = lax.ppermute(initial, axis, down)  10.1 us
  transfers between devices with their start and end apart: 10, of which 3 were waited for; matrix products, arithmetic and copies ran while one was open for 11% of the time, Pallas kernels for 0%

profile of v1, /device:TPU:0, one launch (start us, length us, event | category | flops | bytes accessed | tf_op | source)
XLA Modules:
  0.0 307.4 jit_solution(2859932578354448934)
XLA Ops:
  8.2 34.9 %psum.21 = f32[8]{0:T(128)S(1)} all-reduce(f32[8]{0:T(128)S(1)} %add_reduce_fusion.2), channel_id=1, replica_groups=mesh['grp'=2,'tile'=8,'wave'=2] {'tile','wave'}, use_global_device_ids=true, to_apply=%region_1.2 | all-reduce | flops 8 | bytes 64 | tf_op jit(solution)/shard_map/psum | solution.py:149
  43.7 1.4 fusion.22
  45.2 4.7 %collective-permute-start.1 = (bf16[1,4,2,8,128]{4,3,1,2,0:T(8,128)(2,1)}, bf16[1,4,2,8,128]{4,3,1,2,0:T(8,128)(2,1)}, u32[]{:S(2)}, u32[]{:S(2)}) collective-permute-start(bf16[1,4,2,8,128]{4,3,1,2,0:T(8,128)(2,1)} %fusion.22), channel_id=1, source_target_pairs={{2,0},{4,2},{6,4},{8,6},{10,8},{12,10},{14,12},{0,14},{3,1},{5,3},... | collective-permute-start | bytes 49160 | tf_op jit(solution)/shard_map/ppermute | solution.py:19
  54.7 1.1 cosine_convert_fusion.1
  56.9 1.1 pad_maximum_fusion.2
  58.7 1.6 gather_fusion
  61.8 1.2 copy.121
  63.1 1.3 pad_maximum_fusion.31
  67.8 1.2 copy.122
  69.9 1.2 dynamic-slice
  75.7 1.5 gather_fusion.1
  78.5 34.4 %reduce-scatter.3.cloned.1.call-done = f32[8,2,1024]{2,0,1:T(8,128)} async-done(((f32[128,2,1024]{2,0,1:T(8,128)}), f32[8,2,1024]{2,0,1:T(8,128)}) %reduce-scatter.3.cloned.1.call-update) | async-done | bytes 65552 | tf_op jit(solution)/shard_map/reduce_scatter | solution.py:132
  113.8 20.7 %all_gather.12 = bf16[128,2,1024]{2,0,1:T(8,128)(2,1)S(1)} all-gather(bf16[8,2,1024]{2,0,1:T(8,128)(2,1)S(1)} %multiply_convert_fusion.1), channel_id=1, replica_groups=mesh['grp'=2,'tile'=8,'wave'=2] {'tile','wave'}, dimensions={0}, use_global_device_ids=true | all-gather | bytes 557056 | tf_op jit(solution)/shard_map/all_gather | solution.py:138
  138.5 2.0 convolution_bitcast_fusion.1
  141.5 1.2 subtract_reduce_fusion.1
  145.3 29.8 %all-reduce.1 = (f32[8]{0:T(128)S(1)}, f32[8]{0:T(128)S(1)}) all-reduce(f32[8]{0:T(128)S(1)} %get-tuple-element.16, f32[8]{0:T(128)S(1)} %get-tuple-element.15), channel_id=1, replica_groups=mesh['grp'=2,'tile'=8,'wave'=2] {'tile','wave'}, use_global_device_ids=true, to_apply=%region_8.10 | all-reduce | flops 16 | bytes 128 | tf_op jit(solution)/shard_map/psum | solution.py:157
  177.0 29.5 %all-reduce = f32[128]{0:T(128)S(1)} all-reduce(f32[128]{0:T(128)S(1)} %dynamic-update-slice), channel_id=2, replica_groups=mesh['grp'=2,'tile'=8,'wave'=2] {'tile','wave'}, use_global_device_ids=true, to_apply=%add | all-reduce | flops 128 | bytes 1024
  206.8 4.7 %collective-permute-start.5 = (bf16[1,4,2,8,128]{4,3,1,2,0:T(8,128)(2,1)S(1)}, bf16[1,4,2,8,128]{4,3,1,2,0:T(8,128)(2,1)S(1)}, u32[]{:S(2)}, u32[]{:S(2)}) collective-permute-start(bf16[1,4,2,8,128]{4,3,1,2,0:T(8,128)(2,1)S(1)} %fusion.20), channel_id=1, source_target_pairs={{2,0},{4,2},{6,4},{8,6},{10,8},{12,10},{14,12},{0,14},{3,1},{5,3},... | collective-permute-start | bytes 49160 | tf_op jit(solution)/shard_map/ppermute | solution.py:19
  214.1 1.1 pad_maximum_fusion.3
  217.6 1.5 gather_fusion.2
  219.8 50.2 %reduce-scatter.5.cloned.1.call-done = f32[8,2,1024]{2,0,1:T(8,128)} async-done(((f32[128,2,1024]{2,0,1:T(8,128)}), f32[8,2,1024]{2,0,1:T(8,128)}) %reduce-scatter.5.cloned.1.call-update) | async-done | bytes 65552 | tf_op jit(solution)/shard_map/reduce_scatter | solution.py:132
  270.9 20.8 %all_gather.15 = bf16[128,2,1024]{2,0,1:T(8,128)(2,1)S(1)} all-gather(bf16[8,2,1024]{2,0,1:T(8,128)(2,1)S(1)} %multiply_convert_fusion), channel_id=1, replica_groups=mesh['grp'=2,'tile'=8,'wave'=2] {'tile','wave'}, dimensions={0}, use_global_device_ids=true | all-gather | bytes 557056 | tf_op jit(solution)/shard_map/all_gather | solution.py:138
  295.4 2.0 convolution_bitcast_fusion
  298.4 1.2 subtract_reduce_fusion
  (202 shorter events, 41.4 us)
Async XLA Ops:
  7.2 70.3 %copy-start = (bf16[1,4,9,2,128,128]{5,4,3,2,1,0:T(8,128)(2,1)S(1)}, bf16[1,4,9,2,128,128]{5,4,3,2,1,0:T(8,128)(2,1)}, u32[]{:S(2)}) copy-start(bf16[1,4,9,2,128,128]{5,4,3,2,1,0:T(8,128)(2,1)} %param.11) | copy-start | bytes 7077892
  7.2 105.7 %reduce-scatter.3.cloned.1.call-start = ((), (), s32[]{:S(2)}) async-start(), calls=%async_computation.2 | async-start | bytes 1114112 | tf_op jit(solution)/shard_map/reduce_scatter | solution.py:132
  43.7 7.0 %copy-start.19 = (f32[8]{0:T(128)}, f32[8]{0:T(128)S(1)}, u32[]{:S(2)}) copy-start(f32[8]{0:T(128)S(1)} %get-tuple-element.68) | copy-start | bytes 100
  45.2 17.9 %collective-permute-start = (bf16[1,4,2,8,128]{4,3,1,2,0:T(8,128)(2,1)}, bf16[1,4,2,8,128]{4,3,1,2,0:T(8,128)(2,1)}, u32[]{:S(2)}, u32[]{:S(2)}) collective-permute-start(bf16[1,4,2,8,128]{4,3,1,2,0:T(8,128)(2,1)} %fusion.22), channel_id=1, source_target_pairs={{0,2},{2,4},{4,6},{6,8},{8,10},{10,12},{12,14},{14,0},{1,3},{3,5},... | collective-permute-start | bytes 49160 | tf_op jit(solution)/shard_map/ppermute | solution.py:18
  45.2 17.9 %collective-permute-start.1 = (bf16[1,4,2,8,128]{4,3,1,2,0:T(8,128)(2,1)}, bf16[1,4,2,8,128]{4,3,1,2,0:T(8,128)(2,1)}, u32[]{:S(2)}, u32[]{:S(2)}) collective-permute-start(bf16[1,4,2,8,128]{4,3,1,2,0:T(8,128)(2,1)} %fusion.22), channel_id=1, source_target_pairs={{2,0},{4,2},{6,4},{8,6},{10,8},{12,10},{14,12},{0,14},{3,1},{5,3},... | collective-permute-start | bytes 49160 | tf_op jit(solution)/shard_map/ppermute | solution.py:19
  53.9 12.4 %copy-start.1 = (f32[512,128]{0,1:T(8,128)}, f32[512,128]{0,1:T(8,128)S(1)}, u32[]{:S(2)}) copy-start(f32[512,128]{0,1:T(8,128)S(1)} %get-tuple-element.64) | copy-start | bytes 786436
  58.0 212.0 %reduce-scatter.5.cloned.1.call-start = ((), (), s32[]{:S(2)}) async-start(), calls=%async_computation.3 | async-start | bytes 1114112 | tf_op jit(solution)/shard_map/reduce_scatter | solution.py:132
  64.4 9.4 %collective-permute-start.2 = (bf16[3,1,2,8,128]{4,3,1,2,0:T(8,128)(2,1)}, bf16[3,1,2,8,128]{4,3,1,2,0:T(8,128)(2,1)}, u32[]{:S(2)}, u32[]{:S(2)}) collective-permute-start(bf16[3,1,2,8,128]{4,3,1,2,0:T(8,128)(2,1)} %get-tuple-element.56), channel_id=1, source_target_pairs={{0,1},{1,0},{2,3},{3,2},{4,5},{5,4},{6,7},{7,6},{8,9},{9,8},{10,11... | collective-permute-start | bytes 36872 | tf_op jit(solution)/shard_map/ppermute | solution.py:18
  67.8 9.4 %copy-start.21 = (pred[4,9]{1,0:T(4,128)(4,1)S(1)}, pred[4,9]{1,0:T(4,128)(4,1)}, u32[]{:S(2)}) copy-start(pred[4,9]{1,0:T(4,128)(4,1)} %and_bitcast_fusion) | copy-start | bytes 112
  69.1 43.8 %copy-start.16 = (f32[8,1,1024]{2,0,1:T(8,128)}, f32[8,1,1024]{2,0,1:T(8,128)S(1)}, u32[]{:S(2)}) copy-start(f32[8,1,1024]{2,0,1:T(8,128)S(1)} %copy.122) | copy-start | bytes 98308
  72.5 2.1 collective-permute-start.3
  134.5 4.0 %copy-start.10 = (bf16[512,128]{0,1:T(8,128)(2,1)S(1)}, bf16[512,128]{0,1:T(8,128)(2,1)}, u32[]{:S(2)}) copy-start(bf16[512,128]{0,1:T(8,128)(2,1)} %copy-done.9) | copy-start | bytes 393220
  141.5 2.0 copy-start.20
  141.5 70.1 %copy-start.2 = (f32[512,128]{0,1:T(8,128)S(1)}, f32[512,128]{0,1:T(8,128)}, u32[]{:S(2)}) copy-start(f32[512,128]{0,1:T(8,128)} %copy-done.1) | copy-start | bytes 786436
  176.8 38.4 %copy-start.12 = (f32[1,4,1,8,128]{4,3,1,2,0:T(8,128)}, f32[1,4,1,8,128]{4,3,1,2,0:T(8,128)S(1)}, u32[]{:S(2)}) copy-start(f32[1,4,1,8,128]{4,3,1,2,0:T(8,128)S(1)} %get-tuple-element.51) | copy-start | bytes 49156
  176.8 38.4 %copy-start.14 = (f32[1,4,1,8,128]{4,3,1,2,0:T(8,128)}, f32[1,4,1,8,128]{4,3,1,2,0:T(8,128)S(1)}, u32[]{:S(2)}) copy-start(f32[1,4,1,8,128]{4,3,1,2,0:T(8,128)S(1)} %get-tuple-element.52) | copy-start | bytes 49156
  206.8 8.4 %collective-permute-start.4 = (bf16[1,4,2,8,128]{4,3,1,2,0:T(8,128)(2,1)S(1)}, bf16[1,4,2,8,128]{4,3,1,2,0:T(8,128)(2,1)S(1)}, u32[]{:S(2)}, u32[]{:S(2)}) collective-permute-start(bf16[1,4,2,8,128]{4,3,1,2,0:T(8,128)(2,1)S(1)} %fusion.20), channel_id=1, source_target_pairs={{0,2},{2,4},{4,6},{6,8},{8,10},{10,12},{12,14},{14,0},{1,3},{3,5},... | collective-permute-start | bytes 49160 | tf_op jit(solution)/shard_map/ppermute | solution.py:18
  206.8 8.4 %collective-permute-start.5 = (bf16[1,4,2,8,128]{4,3,1,2,0:T(8,128)(2,1)S(1)}, bf16[1,4,2,8,128]{4,3,1,2,0:T(8,128)(2,1)S(1)}, u32[]{:S(2)}, u32[]{:S(2)}) collective-permute-start(bf16[1,4,2,8,128]{4,3,1,2,0:T(8,128)(2,1)S(1)} %fusion.20), channel_id=1, source_target_pairs={{2,0},{4,2},{6,4},{8,6},{10,8},{12,10},{14,12},{0,14},{3,1},{5,3},... | collective-permute-start | bytes 49160 | tf_op jit(solution)/shard_map/ppermute | solution.py:19
  215.2 4.0 %copy-start.22 = (pred[4,9]{1,0:T(4,128)(4,1)S(1)}, pred[4,9]{1,0:T(4,128)(4,1)}, u32[]{:S(2)}) copy-start(pred[4,9]{1,0:T(4,128)(4,1)} %and_bitcast_fusion) | copy-start | bytes 112
  215.3 1.2 collective-permute-start.7
  215.9 1.3 collective-permute-start.6
  219.1 50.9 %copy-start.17 = (f32[8,1,1024]{2,0,1:T(8,128)S(1)}, f32[8,1,1024]{2,0,1:T(8,128)}, u32[]{:S(2)}) copy-start(f32[8,1,1024]{2,0,1:T(8,128)} %copy-done.16) | copy-start | bytes 98308
  291.7 3.8 %copy-start.11 = (bf16[512,128]{0,1:T(8,128)(2,1)S(1)}, bf16[512,128]{0,1:T(8,128)(2,1)}, u32[]{:S(2)}) copy-start(bf16[512,128]{0,1:T(8,128)(2,1)} %copy-done.9) | copy-start | bytes 393220
  298.4 1.4 copy-start.15
  (11 other events, 11.6 us)
Sparse Core Ops, SparseCore 0:
  58.1 54.7 reduce-scatter.2
  215.3 54.6 reduce-scatter.4
